TPU v7x, 512 devices: a whole 4x4x16 slice. The times are simulated.
512 devices in a mesh: tm: 128 (over x_lo, z, y), feat: 4 (over x_hi, core).
Axes of the slice: x: 4 (x_hi: 2, x_lo: 2; x = x_hi * 2 + x_lo), y: 4, z: 16, core: 2. Of those that a mesh axis runs over, the one named last changes fastest.
Arguments:
- frames: bfloat16 [4096, 2048], P('tm'), may hold values from -6 to 6
- frequency: bfloat16 [2048, 4096], P(None, 'feat'), may hold values from -0.125 to 0.125
- phases: float32 [4096], P('feat'), may hold values from -3.140625 to 3.140625
Outputs:
- instant_tiles: float32 [128, 4, 128, 256], P('tm', 'feat')
- lagged_tiles: float32 [128, 4, 128, 256], P('tm', 'feat')
All inputs are finite; a program needn't handle non-finite values.
Results may differ from a plain program's by a relative error of at most 0.0003.
Values may be sent and summed in bfloat16 or wider, within the bound.
A program may use at most 64 MiB of HBM per device.

v0:
```python
import math
import jax
import jax.numpy as jnp
from jax import lax
from jax.sharding import PartitionSpec as P

LAG = 512
ROW_SPLIT = 8
SCALE = math.sqrt(2.0)


def shards(frames, frequency, phases):
    tm_count = lax.axis_size("tm")
    feat_count = lax.axis_size("feat")
    projected = jnp.dot(frames, frequency, preferred_element_type=jnp.float32) + phases[None, :]
    local_feats = (SCALE * jnp.cos(projected)).astype(jnp.bfloat16)
    frame_count, local_width = local_feats.shape
    feat_width = local_width * feat_count
    tile_rows = feat_width // (feat_count * ROW_SPLIT)
    tile_cols = feat_width * ROW_SPLIT // tm_count
    col_groups = tm_count // ROW_SPLIT
    frame_total = frame_count * tm_count
    all_feats = lax.all_gather(local_feats, "feat", axis=1, tiled=True)
    row_parts = local_feats.reshape(frame_count, ROW_SPLIT, tile_rows).transpose(1, 0, 2)
    row_send = jnp.broadcast_to(row_parts[None], (col_groups, ROW_SPLIT, frame_count, tile_rows))
    row_send = row_send.reshape(tm_count, frame_count, tile_rows)
    row_recv = lax.all_to_all(row_send, "tm", split_axis=0, concat_axis=0, tiled=True).reshape(
        frame_total, tile_rows
    )
    head_rows = row_recv[: frame_total - LAG]
    row_total = all_feats.shape[0]
    col_parts = all_feats.reshape(row_total, col_groups, tile_cols).transpose(1, 0, 2)
    spread_out = jnp.broadcast_to(col_parts[:, None], (col_groups, ROW_SPLIT, row_total, tile_cols))
    received = lax.all_to_all(
        spread_out.reshape(tm_count, row_total, tile_cols),
        "tm",
        split_axis=0,
        concat_axis=0,
        tiled=True,
    )
    col_data = received.reshape(frame_total, received.shape[2])
    instant = (
        jnp.einsum("sr,sc->rc", row_recv, col_data, preferred_element_type=jnp.float32)
        / frame_total
    )
    lagged = jnp.einsum(
        "sr,sc->rc", head_rows, col_data[LAG:], preferred_element_type=jnp.float32
    ) / (frame_total - LAG)
    instant, lagged = (instant, lagged)
    return (instant.reshape(1, 1, tile_rows, tile_cols), lagged.reshape(1, 1, tile_rows, tile_cols))


def solution(mesh):
    placed = (P("tm", None), P(None, "feat"), P("feat"))
    return jax.shard_map(
        shards,
        mesh=mesh,
        in_specs=placed,
        out_specs=(P("tm", "feat", None, None), P("tm", "feat", None, None)),
        check_vma=False,
    )
```

profile of v0, /device:TPU:4, one launch (start us, length us, event | category | flops | bytes accessed | tf_op | source)
XLA Modules:
  0.0 197.1 jit_solution(6521872163242553725)
XLA Ops:
  0.6 0.0 copy-start
  0.6 0.9 copy-done
  1.5 3.4 %fusion.15 = bf16[32,1024]{1,0:T(8,128)(2,1)S(1)} fusion(bf16[32,2048]{1,0:T(8,128)(2,1)S(1)} %copy-done, bf16[2048,1024]{1,0:T(8,128)(2,1)} %param.4, f32[1024]{0:T(1024)} %param.5), kind=kOutput, calls=%fused_computation.11 | convolution fusion | flops 134316032 | bytes 4395008 | tf_op jit(solution)/shard_map/dot_general | solution.py:15
  5.0 1.2 broadcast_in_dim.4
  6.2 20.6 %all-to-all-start = ((bf16[128,32,128]{2,1,0:T(8,128)(2,1)}), bf16[128,32,128]{2,1,0:T(8,128)(2,1)S(1)}, u32[]{:S(2)}, u32[]{:S(2)}) async-start(bf16[128,32,128]{2,1,0:T(8,128)(2,1)} %bitcast.1), calls=%async_computation | async-start | bytes 2097152 | tf_op jit(solution)/shard_map/all_to_all | solution.py:27
  26.8 7.5 %all_gather.3 = bf16[32,4096]{1,0:T(8,128)(2,1)S(1)} all-gather(bf16[32,1024]{1,0:T(8,128)(2,1)S(1)} %fusion.15), channel_id=1, replica_groups=mesh['tm'=128,'feat'=4] {'feat'}, dimensions={1}, use_global_device_ids=true | all-gather | bytes 327680 | tf_op jit(solution)/shard_map/all_gather | solution.py:23
  34.3 0.1 copy.11
  34.4 49.9 %all-to-all-done = bf16[128,32,128]{2,1,0:T(8,128)(2,1)S(1)} async-done(((bf16[128,32,128]{2,1,0:T(8,128)(2,1)}), bf16[128,32,128]{2,1,0:T(8,128)(2,1)S(1)}, u32[]{:S(2)}, u32[]{:S(2)}) %all-to-all-start) | async-done | bytes 1048608 | tf_op jit(solution)/shard_map/all_to_all | solution.py:27
  84.3 0.0 copy-start.1
  84.3 1.7 broadcast_in_dim.5
  86.0 6.2 %all-to-all-start.1 = ((bf16[128,32,256]{2,1,0:T(8,128)(2,1)}), bf16[128,32,256]{2,1,0:T(8,128)(2,1)S(1)}, u32[]{:S(2)}, u32[]{:S(2)}) async-start(bf16[128,32,256]{2,1,0:T(8,128)(2,1)} %bitcast.30), calls=%async_computation.1 | async-start | bytes 4194304 | tf_op jit(solution)/shard_map/all_to_all | solution.py:34
  92.2 0.0 copy-done.1
  92.2 0.0 slice-start
  92.2 100.4 %all-to-all-done.1 = bf16[128,32,256]{2,1,0:T(8,128)(2,1)S(1)} async-done(((bf16[128,32,256]{2,1,0:T(8,128)(2,1)}), bf16[128,32,256]{2,1,0:T(8,128)(2,1)S(1)}, u32[]{:S(2)}, u32[]{:S(2)}) %all-to-all-start.1) | async-done | bytes 2097184 | tf_op jit(solution)/shard_map/all_to_all | solution.py:34
  192.6 0.1 slice.11
  192.8 0.0 slice-done
  192.8 0.0 copy-start.2
  192.8 3.1 %fusion.12 = f32[1,1,128,256]{3,2,1,0:T(8,128)} fusion(bf16[112,32,256]{2,1,0:T(8,128)(2,1)S(1)} %slice.11, bf16[112,32,128]{2,1,0:T(8,128)(2,1)S(1)} %slice-done), kind=kOutput, calls=%fused_computation.10 | convolution fusion | flops 234913792 | bytes 2883584 | tf_op jit(solution)/shard_map/sr,sc->rc/dot_general | solution.py:46
  195.9 0.0 copy-done.2
  195.9 1.2 fusion.8
  (3 shorter events, 0.1 us)
Async XLA Ops:
  0.6 0.9 copy-start
  6.2 78.2 %all-to-all-start = ((bf16[128,32,128]{2,1,0:T(8,128)(2,1)}), bf16[128,32,128]{2,1,0:T(8,128)(2,1)S(1)}, u32[]{:S(2)}, u32[]{:S(2)}) async-start(bf16[128,32,128]{2,1,0:T(8,128)(2,1)} %bitcast.1), calls=%async_computation | async-start | bytes 2097152 | tf_op jit(solution)/shard_map/all_to_all | solution.py:27
  84.3 7.9 %copy-start.1 = (bf16[128,32,128]{2,1,0:T(8,128)(2,1)}, bf16[128,32,128]{2,1,0:T(8,128)(2,1)S(1)}, u32[]{:S(2)}) copy-start(bf16[128,32,128]{2,1,0:T(8,128)(2,1)S(1)} %all-to-all-done) | copy-start | bytes 3145732
  86.0 106.6 %all-to-all-start.1 = ((bf16[128,32,256]{2,1,0:T(8,128)(2,1)}), bf16[128,32,256]{2,1,0:T(8,128)(2,1)S(1)}, u32[]{:S(2)}, u32[]{:S(2)}) async-start(bf16[128,32,256]{2,1,0:T(8,128)(2,1)} %bitcast.30), calls=%async_computation.1 | async-start | bytes 4194304 | tf_op jit(solution)/shard_map/all_to_all | solution.py:34
  92.2 100.6 %slice-start = ((bf16[128,32,128]{2,1,0:T(8,128)(2,1)}), bf16[112,32,128]{2,1,0:T(8,128)(2,1)S(1)}, s32[]{:S(2)}) async-start(bf16[128,32,128]{2,1,0:T(8,128)(2,1)} %copy-done.1), calls=%async_computation.2 | async-start | bytes 1835008 | tf_op jit(solution)/shard_map/slice | solution.py:30
  192.8 3.1 %copy-start.2 = (bf16[128,32,128]{2,1,0:T(8,128)(2,1)S(1)}, bf16[128,32,128]{2,1,0:T(8,128)(2,1)}, u32[]{:S(2)}) copy-start(bf16[128,32,128]{2,1,0:T(8,128)(2,1)} %copy-done.1) | copy-start | bytes 3145732
where the time goes:
time: 197 us
  waiting for transfers between devices  150 us (76%)
  starting transfers between devices  26.8 us (14%)
  matrix products  7.72 us (4%)
  blocking collectives  7.49 us (4%)
  local copies, waits for them, and re-layouts  4.04 us (2%)
    all_to_all x1, waiting for transfers between devices, shards(): lax.all_to_all(spread_out.reshape(tm_count, row_total, tile_cols), 'tm',...  100 us
    all_to_all x1, waiting for transfers between devices, shards(): lax.all_to_all(row_send, 'tm', split_axis=0, concat_axis=0, tiled=True)  49.9 us
    all_to_all x1, starting transfers between devices, shards(): lax.all_to_all(row_send, 'tm', split_axis=0, concat_axis=0, tiled=True)  20.6 us
    all_gather x1, blocking collectives, shards(): all_feats = lax.all_gather(local_feats, 'feat', axis=1, tiled=True)  7.49 us
    all_to_all x1, starting transfers between devices, shards(): lax.all_to_all(spread_out.reshape(tm_count, row_total, tile_cols), 'tm',...  6.21 us
  transfers between devices with their start and end apart: 2, of which 2 were waited for; matrix products, arithmetic and copies ran while one was open for 0% of the time, Pallas kernels for 0%

commit v1 on v0

--- a/solution.py
+++ b/solution.py
@@ -20,7 +20,9 @@
     tile_cols = feat_width * ROW_SPLIT // tm_count
     col_groups = tm_count // ROW_SPLIT
     frame_total = frame_count * tm_count
-    all_feats = lax.all_gather(local_feats, "feat", axis=1, tiled=True)
+    all_feats = jnp.concatenate(
+        lax.all_to_all(jnp.stack([local_feats] * lax.axis_size("feat")), "feat", 0, 0), axis=1
+    )
     row_parts = local_feats.reshape(frame_count, ROW_SPLIT, tile_rows).transpose(1, 0, 2)
     row_send = jnp.broadcast_to(row_parts[None], (col_groups, ROW_SPLIT, frame_count, tile_rows))
     row_send = row_send.reshape(tm_count, frame_count, tile_rows)

time: 197 us -> 208 us (1.056)
  the two profiles are of different devices: /device:TPU:4 before, /device:TPU:2 now
where the time goes in v1:
time: 208 us; the launch traced here: 207 us
  waiting for transfers between devices  162 us (78%)
  starting transfers between devices  31.8 us (15%)
  matrix products  7.72 us (4%)
  local copies, waits for them, and re-layouts  5.11 us (2%)
    all_to_all x1, waiting for transfers between devices, shards(): lax.all_to_all(spread_out.reshape(tm_count, row_total, tile_cols), 'tm',...  98.8 us
    all_to_all x1, waiting for transfers between devices, shards(): lax.all_to_all(row_send, 'tm', split_axis=0, concat_axis=0, tiled=True)  55.6 us
    all_to_all x1, starting transfers between devices, shards(): lax.all_to_all(row_send, 'tm', split_axis=0, concat_axis=0, tiled=True)  20.8 us
    all_to_all x1, starting transfers between devices, shards(): lax.all_to_all(spread_out.reshape(tm_count, row_total, tile_cols), 'tm',...  7.53 us
    all_to_all x1, waiting for transfers between devices, shards(): lax.all_to_all(jnp.stack([local_feats] * lax.axis_size('feat')), 'feat',...  7.48 us
  transfers between devices with their start and end apart: 3, of which 3 were waited for; matrix products, arithmetic and copies ran while one was open for 0% of the time, Pallas kernels for 0%

profile of v1, /device:TPU:2, one launch (start us, length us, event | category | flops | bytes accessed | tf_op | source)
XLA Modules:
  0.0 207.2 jit_solution(9749326742258321993)
XLA Ops:
  0.6 0.0 copy-start
  0.6 0.9 copy-done
  1.5 3.4 %fusion.15 = bf16[32,1024]{1,0:T(8,128)(2,1)S(1)} fusion(bf16[32,2048]{1,0:T(8,128)(2,1)S(1)} %copy-done, bf16[2048,1024]{1,0:T(8,128)(2,1)} %param.4, f32[1024]{0:T(1024)} %param.5), kind=kOutput, calls=%fused_computation.11 | convolution fusion | flops 134316032 | bytes 4395008 | tf_op jit(solution)/shard_map/dot_general | solution.py:15
  5.0 0.7 stack.2
  5.7 3.4 %all-to-all-start.1 = ((bf16[4,32,1024]{2,1,0:T(8,128)(2,1)}), bf16[4,32,1024]{2,1,0:T(8,128)(2,1)S(1)}, u32[]{:S(2)}, u32[]{:S(2)}) async-start(bf16[4,32,1024]{2,1,0:T(8,128)(2,1)} %stack.2), calls=%async_computation.1 | async-start | bytes 524288 | tf_op jit(solution)/shard_map/all_to_all | solution.py:24
  9.2 7.5 %all-to-all-done.1 = bf16[4,32,1024]{2,1,0:T(8,128)(2,1)S(1)} async-done(((bf16[4,32,1024]{2,1,0:T(8,128)(2,1)}), bf16[4,32,1024]{2,1,0:T(8,128)(2,1)S(1)}, u32[]{:S(2)}, u32[]{:S(2)}) %all-to-all-start.1) | async-done | bytes 262176 | tf_op jit(solution)/shard_map/all_to_all | solution.py:24
  16.6 1.2 broadcast_in_dim.4
  17.8 20.8 %all-to-all-start = ((bf16[128,32,128]{2,1,0:T(8,128)(2,1)}), bf16[128,32,128]{2,1,0:T(8,128)(2,1)S(1)}, u32[]{:S(2)}, u32[]{:S(2)}) async-start(bf16[128,32,128]{2,1,0:T(8,128)(2,1)} %bitcast.1), calls=%async_computation | async-start | bytes 2097152 | tf_op jit(solution)/shard_map/all_to_all | solution.py:29
  38.7 0.2 copy.16
  38.9 0.2 reshape_reshape.3
  39.1 0.1 copy.17
  39.2 55.6 %all-to-all-done = bf16[128,32,128]{2,1,0:T(8,128)(2,1)S(1)} async-done(((bf16[128,32,128]{2,1,0:T(8,128)(2,1)}), bf16[128,32,128]{2,1,0:T(8,128)(2,1)S(1)}, u32[]{:S(2)}, u32[]{:S(2)}) %all-to-all-start) | async-done | bytes 1048608 | tf_op jit(solution)/shard_map/all_to_all | solution.py:29
  94.7 0.0 copy-start.1
  94.7 1.6 broadcast_in_dim.5
  96.4 7.5 %all-to-all-start.2 = ((bf16[128,32,256]{2,1,0:T(8,128)(2,1)}), bf16[128,32,256]{2,1,0:T(8,128)(2,1)S(1)}, u32[]{:S(2)}, u32[]{:S(2)}) async-start(bf16[128,32,256]{2,1,0:T(8,128)(2,1)} %bitcast.28), calls=%async_computation.2 | async-start | bytes 4194304 | tf_op jit(solution)/shard_map/all_to_all | solution.py:36
  103.9 0.0 copy-done.1
  103.9 0.0 slice-start
  103.9 98.8 %all-to-all-done.2 = bf16[128,32,256]{2,1,0:T(8,128)(2,1)S(1)} async-done(((bf16[128,32,256]{2,1,0:T(8,128)(2,1)}), bf16[128,32,256]{2,1,0:T(8,128)(2,1)S(1)}, u32[]{:S(2)}, u32[]{:S(2)}) %all-to-all-start.2) | async-done | bytes 2097184 | tf_op jit(solution)/shard_map/all_to_all | solution.py:36
  202.7 0.1 slice.11
  202.9 0.0 slice-done
  202.9 0.0 copy-start.2
  202.9 3.1 %fusion.12 = f32[1,1,128,256]{3,2,1,0:T(8,128)} fusion(bf16[112,32,256]{2,1,0:T(8,128)(2,1)S(1)} %slice.11, bf16[112,32,128]{2,1,0:T(8,128)(2,1)S(1)} %slice-done), kind=kOutput, calls=%fused_computation.10 | convolution fusion | flops 234913792 | bytes 2883584 | tf_op jit(solution)/shard_map/sr,sc->rc/dot_general | solution.py:48
  206.0 0.0 copy-done.2
  206.0 1.2 fusion.8
  (2 shorter events, 0.0 us)
Async XLA Ops:
  0.6 0.9 copy-start
  5.7 10.9 %all-to-all-start.1 = ((bf16[4,32,1024]{2,1,0:T(8,128)(2,1)}), bf16[4,32,1024]{2,1,0:T(8,128)(2,1)S(1)}, u32[]{:S(2)}, u32[]{:S(2)}) async-start(bf16[4,32,1024]{2,1,0:T(8,128)(2,1)} %stack.2), calls=%async_computation.1 | async-start | bytes 524288 | tf_op jit(solution)/shard_map/all_to_all | solution.py:24
  17.8 76.9 %all-to-all-start = ((bf16[128,32,128]{2,1,0:T(8,128)(2,1)}), bf16[128,32,128]{2,1,0:T(8,128)(2,1)S(1)}, u32[]{:S(2)}, u32[]{:S(2)}) async-start(bf16[128,32,128]{2,1,0:T(8,128)(2,1)} %bitcast.1), calls=%async_computation | async-start | bytes 2097152 | tf_op jit(solution)/shard_map/all_to_all | solution.py:29
  94.7 9.2 %copy-start.1 = (bf16[128,32,128]{2,1,0:T(8,128)(2,1)}, bf16[128,32,128]{2,1,0:T(8,128)(2,1)S(1)}, u32[]{:S(2)}) copy-start(bf16[128,32,128]{2,1,0:T(8,128)(2,1)S(1)} %all-to-all-done) | copy-start | bytes 3145732
  96.4 106.3 %all-to-all-start.2 = ((bf16[128,32,256]{2,1,0:T(8,128)(2,1)}), bf16[128,32,256]{2,1,0:T(8,128)(2,1)S(1)}, u32[]{:S(2)}, u32[]{:S(2)}) async-start(bf16[128,32,256]{2,1,0:T(8,128)(2,1)} %bitcast.28), calls=%async_computation.2 | async-start | bytes 4194304 | tf_op jit(solution)/shard_map/all_to_all | solution.py:36
  103.9 98.9 %slice-start = ((bf16[128,32,128]{2,1,0:T(8,128)(2,1)}), bf16[112,32,128]{2,1,0:T(8,128)(2,1)S(1)}, s32[]{:S(2)}) async-start(bf16[128,32,128]{2,1,0:T(8,128)(2,1)} %copy-done.1), calls=%async_computation.3 | async-start | bytes 1835008 | tf_op jit(solution)/shard_map/slice | solution.py:32
  202.9 3.1 %copy-start.2 = (bf16[128,32,128]{2,1,0:T(8,128)(2,1)S(1)}, bf16[128,32,128]{2,1,0:T(8,128)(2,1)}, u32[]{:S(2)}) copy-start(bf16[128,32,128]{2,1,0:T(8,128)(2,1)} %copy-done.1) | copy-start | bytes 3145732
